TPU v7x, 512 devices: a whole 4x8x8 slice. The times are simulated.
512 devices in a mesh: dp: 4 (over y_lo), seq: 32 (over z, y_hi, core), tensor: 4 (over x).
Axes of the slice: x: 4, y: 8 (y_hi: 2, y_lo: 4; y = y_hi * 4 + y_lo), z: 8, core: 2. Of those that a mesh axis runs over, the one named last changes fastest.
Arguments:
- queries: bfloat16 [4, 16384, 512], P('dp', 'seq', 'tensor'), may hold values from -6 to 6
- values: bfloat16 [4, 16384, 512], P('dp', 'seq', 'tensor'), may hold values from -6 to 6
- filt: float32 [16384, 512], P('seq', 'tensor'), may hold values from -4 to 4
- w_out: bfloat16 [512, 4096], P('tensor'), may hold values from -0.375 to 0.375
- cotangent: bfloat16 [4, 16384, 4096], P('dp', 'seq', 'tensor'), may hold values from -6 to 6
Outputs:
- mixed: bfloat16 [4, 16384, 4096], P('dp', 'seq', 'tensor')
- grad_query: bfloat16 [4, 16384, 512], P('dp', 'seq', 'tensor')
- grad_value: bfloat16 [4, 16384, 512], P('dp', 'seq', 'tensor')
- grad_filt: float32 [16384, 512], P('seq', 'tensor')
All inputs are finite; a program needn't handle non-finite values.
Results may differ from a plain program's by a relative error of at most 0.024.
Values may be sent and summed in bfloat16 or wider, within the bound.
No kernel may reach another device: no remote copies, remote signals or barrier semaphores. Data moves between devices by JAX's collectives and lax.ppermute only.
A program may use at most 64 MiB of HBM per device.

v0:
```python
import math
import jax
import jax.numpy as jnp
from jax import lax
from jax.sharding import PartitionSpec as P

HIGHEST = lax.Precision.HIGHEST


def for_sending(array):
    return jax.tree.map(lambda a: a.astype(jnp.bfloat16) if a.dtype == jnp.float32 else a, array)


def angle_table(first, second, period):
    index = first[:, None] * second[None, :] % period
    angle = -2.0 * math.pi / period * index.astype(jnp.float32)
    return (jnp.cos(angle), jnp.sin(angle))


def product(table_real, table_imag, data_real, data_imag, form):

    def apply(left, right):
        return jnp.einsum(form, left, right, precision=HIGHEST)

    return (
        apply(table_real, data_real) - apply(table_imag, data_imag),
        apply(table_real, data_imag) + apply(table_imag, data_real),
    )


def split_length(length):
    levels = length.bit_length() - 1
    inner = 1 << levels // 2
    return (inner, length // inner)


def local_forward(data_real, data_imag, freq_index, total):
    pair, length, width = data_real.shape
    inner, outer = split_length(length)
    cos_t, sin_t = angle_table(freq_index, jnp.arange(length, dtype=jnp.int32), total)
    cos_t = cos_t[:, :, None]
    sin_t = sin_t[:, :, None]
    data_real, data_imag = (
        data_real * cos_t - data_imag * sin_t,
        data_real * sin_t + data_imag * cos_t,
    )
    data_real = data_real.reshape(pair, outer, inner, width)
    data_imag = data_imag.reshape(pair, outer, inner, width)
    outer_c, outer_s = angle_table(
        jnp.arange(outer, dtype=jnp.int32), jnp.arange(outer, dtype=jnp.int32), outer
    )
    data_real, data_imag = product(outer_c, outer_s, data_real, data_imag, "ab,ebcd->eacd")
    mid_c, mid_s = angle_table(
        jnp.arange(outer, dtype=jnp.int32), jnp.arange(inner, dtype=jnp.int32), length
    )
    mid_c = mid_c[None, :, :, None]
    mid_s = mid_s[None, :, :, None]
    data_real, data_imag = (
        data_real * mid_c - data_imag * mid_s,
        data_real * mid_s + data_imag * mid_c,
    )
    inner_c, inner_s = angle_table(
        jnp.arange(inner, dtype=jnp.int32), jnp.arange(inner, dtype=jnp.int32), inner
    )
    return product(inner_c, inner_s, data_real, data_imag, "ab,ecbd->ecad")


def local_inverse(spec_real, spec_imag, freq_index, total):
    pair, outer, inner, width = spec_real.shape
    length = outer * inner
    inner_c, inner_s = angle_table(
        jnp.arange(inner, dtype=jnp.int32), jnp.arange(inner, dtype=jnp.int32), inner
    )
    data_real, data_imag = product(
        inner_c / inner, -inner_s / inner, spec_real, spec_imag, "ab,ecbd->ecad"
    )
    mid_c, mid_s = angle_table(
        jnp.arange(outer, dtype=jnp.int32), jnp.arange(inner, dtype=jnp.int32), length
    )
    mid_c = mid_c[None, :, :, None]
    mid_s = mid_s[None, :, :, None]
    data_real, data_imag = (
        data_real * mid_c + data_imag * mid_s,
        data_imag * mid_c - data_real * mid_s,
    )
    outer_c, outer_s = angle_table(
        jnp.arange(outer, dtype=jnp.int32), jnp.arange(outer, dtype=jnp.int32), outer
    )
    data_real, data_imag = product(
        outer_c / outer, -outer_s / outer, data_real, data_imag, "ab,ebcd->eacd"
    )
    data_real = data_real.reshape(pair, length, width)
    data_imag = data_imag.reshape(pair, length, width)
    cos_t, sin_t = angle_table(freq_index, jnp.arange(length, dtype=jnp.int32), total)
    cos_t = cos_t[:, :, None]
    sin_t = sin_t[:, :, None]
    return (data_real * cos_t + data_imag * sin_t, data_imag * cos_t - data_real * sin_t)


def forward_transform(signal):
    count = lax.axis_size("seq")
    place = lax.axis_index("seq")
    length, width = signal.shape
    total = 2 * count * length
    pieces = lax.all_to_all(
        signal.reshape(count, length // count, width).astype(jnp.bfloat16),
        "seq",
        split_axis=0,
        concat_axis=0,
        tiled=True,
    ).astype(jnp.float32)
    cos_t, sin_t = angle_table(
        jnp.arange(2 * count, dtype=jnp.int32), jnp.arange(count, dtype=jnp.int32), 2 * count
    )
    mixed_real = jnp.einsum("ka,arc->krc", cos_t, pieces, precision=HIGHEST)
    mixed_imag = jnp.einsum("ka,arc->krc", sin_t, pieces, precision=HIGHEST)
    mixed_real, mixed_imag = (
        lax.all_to_all(
            for_sending(mixed_real), "seq", split_axis=0, concat_axis=1, tiled=True
        ).astype(mixed_real.dtype),
        lax.all_to_all(
            for_sending(mixed_imag), "seq", split_axis=0, concat_axis=1, tiled=True
        ).astype(mixed_imag.dtype),
    )
    freq_index = 2 * place + jnp.arange(2, dtype=jnp.int32)
    return (local_forward(mixed_real, mixed_imag, freq_index, total), freq_index)


def inverse_transform(spectrum, freq_index):
    count = lax.axis_size("seq")
    pair, outer, inner, width = spectrum[0].shape
    length = outer * inner
    total = 2 * count * length
    data_real, data_imag = local_inverse(spectrum[0], spectrum[1], freq_index, total)
    part_real, part_imag = (
        lax.all_to_all(
            for_sending(data_real), "seq", split_axis=1, concat_axis=0, tiled=True
        ).astype(data_real.dtype),
        lax.all_to_all(
            for_sending(data_imag), "seq", split_axis=1, concat_axis=0, tiled=True
        ).astype(data_imag.dtype),
    )
    cos_t, sin_t = angle_table(
        jnp.arange(2 * count, dtype=jnp.int32), jnp.arange(count, dtype=jnp.int32), 2 * count
    )
    signal = (
        jnp.einsum("ka,krc->arc", cos_t, part_real, precision=HIGHEST)
        + jnp.einsum("ka,krc->arc", sin_t, part_imag, precision=HIGHEST)
    ) / (2 * count)
    signal = lax.all_to_all(
        for_sending(signal), "seq", split_axis=0, concat_axis=0, tiled=True
    ).astype(signal.dtype)
    return signal.reshape(length, width)


def split_spec(spectrum, width):
    first = (spectrum[0][..., :width], spectrum[1][..., :width])
    second = (spectrum[0][..., width:], spectrum[1][..., width:])
    return (first, second)


def times_spec(left, right):
    return (left[0] * right[0] - left[1] * right[1], left[0] * right[1] + left[1] * right[0])


def conj_times(left, right):
    return (left[0] * right[0] + left[1] * right[1], left[0] * right[1] - left[1] * right[0])


def per_device(queries, values, filt, w_out, cotangent):
    query = queries[0].astype(jnp.float32)
    value = values[0].astype(jnp.float32)
    width = filt.shape[1]
    joined = jnp.concatenate([value, filt], axis=1)
    spectrum, freq_index = forward_transform(joined)
    value_spec, filt_spec = split_spec(spectrum, width)
    conv = inverse_transform(times_spec(value_spec, filt_spec), freq_index)
    gated = (query * conv).astype(jnp.bfloat16)
    partial_sum = jnp.dot(gated, w_out, preferred_element_type=jnp.float32)
    mixed = lax.psum_scatter(
        partial_sum.astype(jnp.bfloat16), "tensor", scatter_dimension=1, tiled=True
    )
    grad_gated = lax.dot_general(
        lax.all_gather(cotangent[0], "tensor", axis=1, tiled=True),
        w_out,
        (((1,), (1,)), ((), ())),
        preferred_element_type=jnp.float32,
    )
    grad_query = (grad_gated * conv).astype(jnp.bfloat16)
    grad_conv = grad_gated * query
    grad_spec = forward_transform(grad_conv)[0]
    back_value = conj_times(filt_spec, grad_spec)
    back_filt = conj_times(value_spec, grad_spec)
    both_spec = (
        jnp.concatenate([back_value[0], back_filt[0]], axis=3),
        jnp.concatenate([back_value[1], back_filt[1]], axis=3),
    )
    result = inverse_transform(both_spec, freq_index)
    grad_value = result[:, :width].astype(jnp.bfloat16)
    grad_filt = lax.psum(result[:, width:].astype(jnp.bfloat16), "dp").astype(jnp.float32)
    return (mixed[None], grad_query[None], grad_value[None], grad_filt)


def solution(mesh):
    placed = (
        P("dp", "seq", "tensor"),
        P("dp", "seq", "tensor"),
        P("seq", "tensor"),
        P("tensor", None),
        P("dp", "seq", "tensor"),
    )
    return jax.shard_map(
        per_device,
        mesh=mesh,
        in_specs=placed,
        out_specs=(
            P("dp", "seq", "tensor"),
            P("dp", "seq", "tensor"),
            P("dp", "seq", "tensor"),
            P("seq", "tensor"),
        ),
        check_vma=False,
    )
```

profile of v0, /device:TPU:1, one launch (start us, length us, event | category | flops | bytes accessed | tf_op | source)
XLA Modules:
  0.0 429.1 jit_solution(16543263097162809174)
XLA Ops:
  7.9 1.0 convert.18
  8.9 0.9 pad_maximum_fusion.6
  9.8 30.7 %all_to_all.128 = bf16[32,16,256]{2,1,0:T(8,128)(2,1)S(1)} all-to-all(bf16[32,16,256]{2,1,0:T(8,128)(2,1)S(1)} %bitcast.303), channel_id=1, replica_groups=mesh['dp'=4,'seq'=32,'tensor'=4] {'seq'}, dimensions={0} | all-to-all | bytes 524288 | tf_op jit(solution)/shard_map/all_to_all | solution.py:105
  41.2 1.1 copy.71
  42.3 5.8 %all-to-all-start.1 = ((bf16[64,16,256]{2,1,0:T(8,128)(2,1)}), bf16[64,16,256]{2,1,0:T(8,128)(2,1)S(1)}, u32[]{:S(2)}, u32[]{:S(2)}) async-start(bf16[64,16,256]{2,1,0:T(8,128)(2,1)} %copy.71), calls=%async_computation.1 | async-start | bytes 1048576 | tf_op jit(solution)/shard_map/all_to_all | solution.py:118
  48.8 1.1 copy.74
  49.9 14.1 %all-to-all-done.1 = bf16[64,16,256]{2,1,0:T(8,128)(2,1)S(1)} async-done(((bf16[64,16,256]{2,1,0:T(8,128)(2,1)}), bf16[64,16,256]{2,1,0:T(8,128)(2,1)S(1)}, u32[]{:S(2)}, u32[]{:S(2)}) %all-to-all-start.1) | async-done | bytes 524320 | tf_op jit(solution)/shard_map/all_to_all | solution.py:118
  64.0 9.6 %all-to-all-start.2 = ((bf16[64,16,256]{2,1,0:T(8,128)(2,1)}), bf16[64,16,256]{2,1,0:T(8,128)(2,1)}, u32[]{:S(2)}, u32[]{:S(2)}) async-start(bf16[64,16,256]{2,1,0:T(8,128)(2,1)} %copy.74), calls=%async_computation.2 | async-start | bytes 1048576 | tf_op jit(solution)/shard_map/all_to_all | solution.py:121
  74.3 15.0 %all-to-all-done.2 = bf16[64,16,256]{2,1,0:T(8,128)(2,1)} async-done(((bf16[64,16,256]{2,1,0:T(8,128)(2,1)}), bf16[64,16,256]{2,1,0:T(8,128)(2,1)}, u32[]{:S(2)}, u32[]{:S(2)}) %all-to-all-start.2) | async-done | bytes 524320 | tf_op jit(solution)/shard_map/all_to_all | solution.py:121
  89.3 1.2 convert.22
  90.5 2.4 fusion.61
  92.9 2.4 fusion.65
  95.2 2.4 fusion.7
  97.7 3.8 multiply_subtract_fusion
  101.5 4.3 fusion.58
  105.8 9.8 %all-to-all-start.6 = ((bf16[32,16,128]{2,1,0:T(8,128)(2,1)}), bf16[32,16,128]{2,1,0:T(8,128)(2,1)S(1)}, u32[]{:S(2)}, u32[]{:S(2)}) async-start(bf16[32,16,128]{2,1,0:T(8,128)(2,1)} %bitcast.55), calls=%async_computation.7 | async-start | bytes 262144 | tf_op jit(solution)/shard_map/all_to_all | solution.py:105
  115.6 2.6 fusion.34
  118.2 9.6 %all-to-all-done.6 = bf16[32,16,128]{2,1,0:T(8,128)(2,1)S(1)} async-done(((bf16[32,16,128]{2,1,0:T(8,128)(2,1)}), bf16[32,16,128]{2,1,0:T(8,128)(2,1)S(1)}, u32[]{:S(2)}, u32[]{:S(2)}) %all-to-all-start.6) | async-done | bytes 131104 | tf_op jit(solution)/shard_map/all_to_all | solution.py:105
  129.2 4.6 %all-to-all-start.7 = ((bf16[64,16,128]{2,1,0:T(8,128)(2,1)}), bf16[64,16,128]{2,1,0:T(8,128)(2,1)}, u32[]{:S(2)}, u32[]{:S(2)}) async-start(bf16[64,16,128]{2,1,0:T(8,128)(2,1)} %copy.96), calls=%async_computation.8 | async-start | bytes 524288 | tf_op jit(solution)/shard_map/all_to_all | solution.py:118
  133.9 3.8 fusion.5
  139.1 8.6 %all-to-all-done.7 = bf16[64,16,128]{2,1,0:T(8,128)(2,1)} async-done(((bf16[64,16,128]{2,1,0:T(8,128)(2,1)}), bf16[64,16,128]{2,1,0:T(8,128)(2,1)}, u32[]{:S(2)}, u32[]{:S(2)}) %all-to-all-start.7) | async-done | bytes 262176 | tf_op jit(solution)/shard_map/all_to_all | solution.py:118
  147.7 5.8 %all-to-all-start.8 = ((bf16[64,16,128]{2,1,0:T(8,128)(2,1)}), bf16[64,16,128]{2,1,0:T(8,128)(2,1)S(1)}, u32[]{:S(2)}, u32[]{:S(2)}) async-start(bf16[64,16,128]{2,1,0:T(8,128)(2,1)} %copy.99), calls=%async_computation.9 | async-start | bytes 524288 | tf_op jit(solution)/shard_map/all_to_all | solution.py:121
  153.5 1.6 fusion.30
  155.1 1.6 fusion.4
  156.8 1.0 convert.23
  157.8 9.4 %all-to-all-done.8 = bf16[64,16,128]{2,1,0:T(8,128)(2,1)S(1)} async-done(((bf16[64,16,128]{2,1,0:T(8,128)(2,1)}), bf16[64,16,128]{2,1,0:T(8,128)(2,1)S(1)}, u32[]{:S(2)}, u32[]{:S(2)}) %all-to-all-start.8) | async-done | bytes 262176 | tf_op jit(solution)/shard_map/all_to_all | solution.py:121
  167.2 1.3 fusion.72
  168.5 1.3 fusion.76
  169.8 1.3 fusion.12
  171.1 1.4 multiply_subtract_fusion.3
  172.6 0.9 fusion.48
  173.5 0.9 fusion.44
  174.4 0.9 fusion.9
  175.3 1.4 multiply_subtract_fusion.2
  177.4 1.1 fusion.36
  178.4 1.1 fusion.37
  179.5 1.1 convolution_add_fusion.1
  180.6 1.4 add_bitcast_fusion
  182.0 1.7 fusion.28
  183.7 1.7 fusion.24
  185.4 1.7 fusion.3
  187.2 1.9 fusion.2
  190.4 1.1 fusion.21
  191.5 1.4 copy.116
  192.9 5.8 %all-to-all-start.10 = ((bf16[2,512,256]{2,0,1:T(2,128)(2,1)}), bf16[2,512,256]{2,0,1:T(2,128)(2,1)S(1)}, u32[]{:S(2)}, u32[]{:S(2)}) async-start(bf16[2,512,256]{2,0,1:T(2,128)(2,1)} %copy.116), calls=%async_computation.11 | async-start | bytes 1048576 | tf_op jit(solution)/shard_map/all_to_all | solution.py:139
  198.7 2.4 copy.113
  203.8 10.6 %all-to-all-done.10 = bf16[2,512,256]{2,0,1:T(2,128)(2,1)S(1)} async-done(((bf16[2,512,256]{2,0,1:T(2,128)(2,1)}), bf16[2,512,256]{2,0,1:T(2,128)(2,1)S(1)}, u32[]{:S(2)}, u32[]{:S(2)}) %all-to-all-start.10) | async-done | bytes 524320 | tf_op jit(solution)/shard_map/all_to_all | solution.py:139
  214.5 9.3 %all-to-all-start.9 = ((bf16[2,512,256]{2,0,1:T(2,128)(2,1)}), bf16[2,512,256]{2,0,1:T(2,128)(2,1)}, u32[]{:S(2)}, u32[]{:S(2)}) async-start(bf16[2,512,256]{2,0,1:T(2,128)(2,1)} %copy.113), calls=%async_computation.10 | async-start | bytes 1048576 | tf_op jit(solution)/shard_map/all_to_all | solution.py:136
  227.1 1.0 copy.91
  228.1 11.6 %all-to-all-done.9 = bf16[2,512,256]{2,0,1:T(2,128)(2,1)} async-done(((bf16[2,512,256]{2,0,1:T(2,128)(2,1)}), bf16[2,512,256]{2,0,1:T(2,128)(2,1)}, u32[]{:S(2)}, u32[]{:S(2)}) %all-to-all-start.9) | async-done | bytes 524320 | tf_op jit(solution)/shard_map/all_to_all | solution.py:136
  239.7 9.6 %all-to-all-start.4 = ((bf16[2,512,128]{2,0,1:T(2,128)(2,1)}), bf16[2,512,128]{2,0,1:T(2,128)(2,1)S(1)}, u32[]{:S(2)}, u32[]{:S(2)}) async-start(bf16[2,512,128]{2,0,1:T(2,128)(2,1)} %copy.91), calls=%async_computation.4 | async-start | bytes 524288 | tf_op jit(solution)/shard_map/all_to_all | solution.py:139
  249.3 1.0 copy.88
  251.1 1.1 copy.114
  253.0 9.8 %all-to-all-done.4 = bf16[2,512,128]{2,0,1:T(2,128)(2,1)S(1)} async-done(((bf16[2,512,128]{2,0,1:T(2,128)(2,1)}), bf16[2,512,128]{2,0,1:T(2,128)(2,1)S(1)}, u32[]{:S(2)}, u32[]{:S(2)}) %all-to-all-start.4) | async-done | bytes 262176 | tf_op jit(solution)/shard_map/all_to_all | solution.py:139
  262.8 5.8 %all-to-all-start.3 = ((bf16[2,512,128]{2,0,1:T(2,128)(2,1)}), bf16[2,512,128]{2,0,1:T(2,128)(2,1)S(1)}, u32[]{:S(2)}, u32[]{:S(2)}) async-start(bf16[2,512,128]{2,0,1:T(2,128)(2,1)} %copy.88), calls=%async_computation.3 | async-start | bytes 524288 | tf_op jit(solution)/shard_map/all_to_all | solution.py:136
  270.4 11.9 %all-to-all-done.3 = bf16[2,512,128]{2,0,1:T(2,128)(2,1)S(1)} async-done(((bf16[2,512,128]{2,0,1:T(2,128)(2,1)}), bf16[2,512,128]{2,0,1:T(2,128)(2,1)S(1)}, u32[]{:S(2)}, u32[]{:S(2)}) %all-to-all-start.3) | async-done | bytes 262176 | tf_op jit(solution)/shard_map/all_to_all | solution.py:136
  282.3 5.8 %all-to-all-start.11 = ((bf16[32,16,256]{2,1,0:T(8,128)(2,1)}), bf16[32,16,256]{2,1,0:T(8,128)(2,1)S(1)}, u32[]{:S(2)}, u32[]{:S(2)}) async-start(bf16[32,16,256]{2,1,0:T(8,128)(2,1)} %copy.119), calls=%async_computation.12 | async-start | bytes 524288 | tf_op jit(solution)/shard_map/all_to_all | solution.py:150
  290.2 11.6 %all-to-all-done.11 = bf16[32,16,256]{2,1,0:T(8,128)(2,1)S(1)} async-done(((bf16[32,16,256]{2,1,0:T(8,128)(2,1)}), bf16[32,16,256]{2,1,0:T(8,128)(2,1)S(1)}, u32[]{:S(2)}, u32[]{:S(2)}) %all-to-all-start.11) | async-done | bytes 262176 | tf_op jit(solution)/shard_map/all_to_all | solution.py:150
  301.8 5.8 %all-to-all-start.5 = ((bf16[32,16,128]{2,1,0:T(8,128)(2,1)}), bf16[32,16,128]{2,1,0:T(8,128)(2,1)S(1)}, u32[]{:S(2)}, u32[]{:S(2)}) async-start(bf16[32,16,128]{2,1,0:T(8,128)(2,1)} %copy.94), calls=%async_computation.5 | async-start | bytes 262144 | tf_op jit(solution)/shard_map/all_to_all | solution.py:150
  308.4 11.5 %all-to-all-done.5 = bf16[32,16,128]{2,1,0:T(8,128)(2,1)S(1)} async-done(((bf16[32,16,128]{2,1,0:T(8,128)(2,1)}), bf16[32,16,128]{2,1,0:T(8,128)(2,1)S(1)}, u32[]{:S(2)}, u32[]{:S(2)}) %all-to-all-start.5) | async-done | bytes 131104 | tf_op jit(solution)/shard_map/all_to_all | solution.py:150
  320.0 3.2 convolution_convert_fusion
  323.9 41.7 %all-reduce.2.cloned.1.call-done = bf16[512,128]{1,0:T(8,128)(2,1)} async-done(((bf16[512,128]{1,0:T(8,128)(2,1)}), bf16[512,128]{1,0:T(8,128)(2,1)}) %all-reduce.2.cloned.1.call-update) | async-done | bytes 131088 | tf_op jit(solution)/shard_map/psum | solution.py:200
  365.7 1.6 convert_element_type.305
  367.3 55.0 %reduce-scatter.2.cloned.1.call-done = bf16[512,1024]{1,0:T(8,128)(2,1)} async-done(((bf16[512,4096]{1,0:T(8,128)(2,1)}), bf16[512,1024]{1,0:T(8,128)(2,1)}) %reduce-scatter.2.cloned.1.call-update) | async-done | bytes 1048592 | tf_op jit(solution)/shard_map/reduce_scatter | solution.py:180
  (64 shorter events, 20.3 us)
Async XLA Ops:
  7.2 94.4 %copy-start = (bf16[128,4096]{1,0:T(8,128)(2,1)S(1)}, bf16[128,4096]{1,0:T(8,128)(2,1)}, u32[]{:S(2)}) copy-start(bf16[128,4096]{1,0:T(8,128)(2,1)} %param.8) | copy-start | bytes 3145732
  7.2 94.3 %all-gather.3.cloned.1.call-start = ((), (), s32[]{:S(2)}) async-start(), calls=%async_computation.15 | async-start | bytes 5242880 | tf_op jit(solution)/shard_map/all_gather | solution.py:184
  42.3 21.7 %all-to-all-start.1 = ((bf16[64,16,256]{2,1,0:T(8,128)(2,1)}), bf16[64,16,256]{2,1,0:T(8,128)(2,1)S(1)}, u32[]{:S(2)}, u32[]{:S(2)}) async-start(bf16[64,16,256]{2,1,0:T(8,128)(2,1)} %copy.71), calls=%async_computation.1 | async-start | bytes 1048576 | tf_op jit(solution)/shard_map/all_to_all | solution.py:118
  64.0 25.3 %all-to-all-start.2 = ((bf16[64,16,256]{2,1,0:T(8,128)(2,1)}), bf16[64,16,256]{2,1,0:T(8,128)(2,1)}, u32[]{:S(2)}, u32[]{:S(2)}) async-start(bf16[64,16,256]{2,1,0:T(8,128)(2,1)} %copy.74), calls=%async_computation.2 | async-start | bytes 1048576 | tf_op jit(solution)/shard_map/all_to_all | solution.py:121
  97.7 3.9 copy-start.4
  101.5 32.4 %copy-start.1 = (f32[2,32,16,256]{3,1,2,0:T(8,128)S(1)}, f32[2,32,16,256]{3,1,2,0:T(8,128)}, u32[]{:S(2)}) copy-start(f32[2,32,16,256]{3,1,2,0:T(8,128)} %get-tuple-element.11) | copy-start | bytes 3145732
  105.8 22.0 %all-to-all-start.6 = ((bf16[32,16,128]{2,1,0:T(8,128)(2,1)}), bf16[32,16,128]{2,1,0:T(8,128)(2,1)S(1)}, u32[]{:S(2)}, u32[]{:S(2)}) async-start(bf16[32,16,128]{2,1,0:T(8,128)(2,1)} %bitcast.55), calls=%async_computation.7 | async-start | bytes 262144 | tf_op jit(solution)/shard_map/all_to_all | solution.py:105
  129.2 18.4 %all-to-all-start.7 = ((bf16[64,16,128]{2,1,0:T(8,128)(2,1)}), bf16[64,16,128]{2,1,0:T(8,128)(2,1)}, u32[]{:S(2)}, u32[]{:S(2)}) async-start(bf16[64,16,128]{2,1,0:T(8,128)(2,1)} %copy.96), calls=%async_computation.8 | async-start | bytes 524288 | tf_op jit(solution)/shard_map/all_to_all | solution.py:118
  147.7 19.5 %all-to-all-start.8 = ((bf16[64,16,128]{2,1,0:T(8,128)(2,1)}), bf16[64,16,128]{2,1,0:T(8,128)(2,1)S(1)}, u32[]{:S(2)}, u32[]{:S(2)}) async-start(bf16[64,16,128]{2,1,0:T(8,128)(2,1)} %copy.99), calls=%async_computation.9 | async-start | bytes 524288 | tf_op jit(solution)/shard_map/all_to_all | solution.py:121
  169.8 5.5 %copy-start.2 = (f32[2,32,16,256]{3,2,1,0:T(8,128)S(1)}, f32[2,32,16,256]{3,2,1,0:T(8,128)}, u32[]{:S(2)}) copy-start(f32[2,32,16,256]{3,2,1,0:T(8,128)} %fusion.5) | copy-start | bytes 3145732
  192.9 21.6 %all-to-all-start.10 = ((bf16[2,512,256]{2,0,1:T(2,128)(2,1)}), bf16[2,512,256]{2,0,1:T(2,128)(2,1)S(1)}, u32[]{:S(2)}, u32[]{:S(2)}) async-start(bf16[2,512,256]{2,0,1:T(2,128)(2,1)} %copy.116), calls=%async_computation.11 | async-start | bytes 1048576 | tf_op jit(solution)/shard_map/all_to_all | solution.py:139
  214.5 25.2 %all-to-all-start.9 = ((bf16[2,512,256]{2,0,1:T(2,128)(2,1)}), bf16[2,512,256]{2,0,1:T(2,128)(2,1)}, u32[]{:S(2)}, u32[]{:S(2)}) async-start(bf16[2,512,256]{2,0,1:T(2,128)(2,1)} %copy.113), calls=%async_computation.10 | async-start | bytes 1048576 | tf_op jit(solution)/shard_map/all_to_all | solution.py:136
  239.7 23.1 %all-to-all-start.4 = ((bf16[2,512,128]{2,0,1:T(2,128)(2,1)}), bf16[2,512,128]{2,0,1:T(2,128)(2,1)S(1)}, u32[]{:S(2)}, u32[]{:S(2)}) async-start(bf16[2,512,128]{2,0,1:T(2,128)(2,1)} %copy.91), calls=%async_computation.4 | async-start | bytes 524288 | tf_op jit(solution)/shard_map/all_to_all | solution.py:139
  253.0 67.0 %copy-start.5 = (bf16[1,512,128]{2,1,0:T(8,128)(2,1)S(1)}, bf16[1,512,128]{2,1,0:T(8,128)(2,1)}, u32[]{:S(2)}) copy-start(bf16[1,512,128]{2,1,0:T(8,128)(2,1)} %param.5) | copy-start | bytes 393220
  262.8 19.5 %all-to-all-start.3 = ((bf16[2,512,128]{2,0,1:T(2,128)(2,1)}), bf16[2,512,128]{2,0,1:T(2,128)(2,1)S(1)}, u32[]{:S(2)}, u32[]{:S(2)}) async-start(bf16[2,512,128]{2,0,1:T(2,128)(2,1)} %copy.88), calls=%async_computation.3 | async-start | bytes 524288 | tf_op jit(solution)/shard_map/all_to_all | solution.py:136
  282.3 19.5 %all-to-all-start.11 = ((bf16[32,16,256]{2,1,0:T(8,128)(2,1)}), bf16[32,16,256]{2,1,0:T(8,128)(2,1)S(1)}, u32[]{:S(2)}, u32[]{:S(2)}) async-start(bf16[32,16,256]{2,1,0:T(8,128)(2,1)} %copy.119), calls=%async_computation.12 | async-start | bytes 524288 | tf_op jit(solution)/shard_map/all_to_all | solution.py:150
  301.8 18.2 %all-to-all-start.5 = ((bf16[32,16,128]{2,1,0:T(8,128)(2,1)}), bf16[32,16,128]{2,1,0:T(8,128)(2,1)S(1)}, u32[]{:S(2)}, u32[]{:S(2)}) async-start(bf16[32,16,128]{2,1,0:T(8,128)(2,1)} %copy.94), calls=%async_computation.5 | async-start | bytes 262144 | tf_op jit(solution)/shard_map/all_to_all | solution.py:150
  307.6 58.1 %all-reduce.2.cloned.1.call-start = ((), (), s32[]{:S(2)}) async-start(), calls=%async_computation.14 | async-start | bytes 262144 | tf_op jit(solution)/shard_map/psum | solution.py:200
  308.4 113.9 %reduce-scatter.2.cloned.1.call-start = ((), (), s32[]{:S(2)}) async-start(), calls=%async_computation.13 | async-start | bytes 5242880 | tf_op jit(solution)/shard_map/reduce_scatter | solution.py:180
  320.0 3.3 copy-start.3
Sparse Core Ops, SparseCore 0:
  10.1 59.0 all-gather.2
  311.4 54.2 all-reduce.1
  369.3 52.8 reduce-scatter.1
where the time goes:
time: 433 us; the launch traced here: 429 us
  waiting for transfers between devices  221 us (51%)
  starting transfers between devices  78.1 us (18%)
  matrix products  59 us (14%)
  blocking collectives  30.7 us (7%)
  local copies, waits for them, and re-layouts  17.2 us (4%)
  between operations  14.6 us (3%)
  other arithmetic  8.43 us (2%)
    reduce_scatter x1, waiting for transfers between devices, per_device(): lax.psum_scatter(partial_sum.astype(jnp.bfloat16), 'tensor', scatter_dime...  55 us
    dot_general x32, matrix products, apply(): return jnp.einsum(form, left, right, precision=HIGHEST)  47.5 us
    psum x1, waiting for transfers between devices, per_device(): lax.psum(result[:, width:].astype(jnp.bfloat16), 'dp').astype(jnp.float32)  41.7 us
    all_to_all x1, blocking collectives, forward_transform(): lax.all_to_all(signal.reshape(count, length // count, width).astype(jnp.b...  30.7 us
    all_to_all x2, waiting for transfers between devices, forward_transform(): lax.all_to_all(for_sending(mixed_imag), 'seq', split_axis=0, concat_axis=...  24.4 us
    all_to_all x2, waiting for transfers between devices, inverse_transform(): lax.all_to_all(for_sending(data_real), 'seq', split_axis=1, concat_axis=0...  23.5 us
    all_to_all x2, waiting for transfers between devices, inverse_transform(): lax.all_to_all(for_sending(signal), 'seq', split_axis=0, concat_axis=0, t...  23.1 us
    all_to_all x2, waiting for transfers between devices, forward_transform(): lax.all_to_all(for_sending(mixed_real), 'seq', split_axis=0, concat_axis=...  22.7 us
  transfers between devices with their start and end apart: 14, of which 13 were waited for; matrix products, arithmetic and copies ran while one was open for 12% of the time, Pallas kernels for 0%

commit v1 on v0

--- a/solution.py
+++ b/solution.py
@@ -197,7 +197,9 @@
     )
     result = inverse_transform(both_spec, freq_index)
     grad_value = result[:, :width].astype(jnp.bfloat16)
-    grad_filt = lax.psum(result[:, width:].astype(jnp.bfloat16), "dp").astype(jnp.float32)
+    grad_filt = jnp.sum(
+        lax.all_gather(result[:, width:].astype(jnp.bfloat16), "dp"), axis=0
+    ).astype(jnp.float32)
     return (mixed[None], grad_query[None], grad_value[None], grad_filt)
 
 

time: 433 us -> 364 us (0.84)
  the two profiles are of different devices: /device:TPU:1 before, /device:TPU:2 now
where the time goes in v1:
time: 364 us; the launch traced here: 360 us
  waiting for transfers between devices  133 us (37%)
  blocking collectives  67 us (18%)
  starting transfers between devices  60.1 us (17%)
  matrix products  60 us (16%)
  local copies, waits for them, and re-layouts  16.4 us (5%)
  between operations  15 us (4%)
  other arithmetic  8.11 us (2%)
    dot_general x32, matrix products, apply(): return jnp.einsum(form, left, right, precision=HIGHEST)  48.6 us
    all_to_all x2, waiting for transfers between devices, inverse_transform(): lax.all_to_all(for_sending(data_real), 'seq', split_axis=1, concat_axis=0...  30.6 us
    all_to_all x1, blocking collectives, forward_transform(): lax.all_to_all(signal.reshape(count, length // count, width).astype(jnp.b...  29.8 us
    all_to_all x2, waiting for transfers between devices, inverse_transform(): lax.all_to_all(for_sending(data_imag), 'seq', split_axis=1, concat_axis=0...  28.6 us
    all_to_all x2, waiting for transfers between devices, forward_transform(): lax.all_to_all(for_sending(mixed_imag), 'seq', split_axis=0, concat_axis=...  25.4 us
    all_to_all x2, waiting for transfers between devices, forward_transform(): lax.all_to_all(for_sending(mixed_real), 'seq', split_axis=0, concat_axis=...  24.7 us
    all_gather x1, blocking collectives, per_device(): lax.all_gather(result[:, width:].astype(jnp.bfloat16), 'dp')  19.2 us
    all_to_all x1, blocking collectives, inverse_transform(): lax.all_to_all(for_sending(signal), 'seq', split_axis=0, concat_axis=0, t...  18 us
  transfers between devices with their start and end apart: 12, of which 10 were waited for; matrix products, arithmetic and copies ran while one was open for 15% of the time, Pallas kernels for 0%

profile of v1, /device:TPU:2, one launch (start us, length us, event | category | flops | bytes accessed | tf_op | source)
XLA Modules:
  0.0 359.8 jit_solution(6267958248809366986)
XLA Ops:
  7.9 1.0 convert.19
  8.9 0.9 pad_maximum_fusion.6
  9.8 29.8 %all_to_all.128 = bf16[32,16,256]{2,1,0:T(8,128)(2,1)S(1)} all-to-all(bf16[32,16,256]{2,1,0:T(8,128)(2,1)S(1)} %bitcast.305), channel_id=1, replica_groups=mesh['dp'=4,'seq'=32,'tensor'=4] {'seq'}, dimensions={0} | all-to-all | bytes 524288 | tf_op jit(solution)/shard_map/all_to_all | solution.py:105
  40.4 1.1 copy.71
  41.4 5.4 %all-to-all-start.1 = ((bf16[64,16,256]{2,1,0:T(8,128)(2,1)}), bf16[64,16,256]{2,1,0:T(8,128)(2,1)S(1)}, u32[]{:S(2)}, u32[]{:S(2)}) async-start(bf16[64,16,256]{2,1,0:T(8,128)(2,1)} %copy.71), calls=%async_computation.1 | async-start | bytes 1048576 | tf_op jit(solution)/shard_map/all_to_all | solution.py:118
  47.6 1.1 copy.74
  48.7 16.1 %all-to-all-done.1 = bf16[64,16,256]{2,1,0:T(8,128)(2,1)S(1)} async-done(((bf16[64,16,256]{2,1,0:T(8,128)(2,1)}), bf16[64,16,256]{2,1,0:T(8,128)(2,1)S(1)}, u32[]{:S(2)}, u32[]{:S(2)}) %all-to-all-start.1) | async-done | bytes 524320 | tf_op jit(solution)/shard_map/all_to_all | solution.py:118
  64.7 7.5 %all-to-all-start.2 = ((bf16[64,16,256]{2,1,0:T(8,128)(2,1)}), bf16[64,16,256]{2,1,0:T(8,128)(2,1)}, u32[]{:S(2)}, u32[]{:S(2)}) async-start(bf16[64,16,256]{2,1,0:T(8,128)(2,1)} %copy.74), calls=%async_computation.2 | async-start | bytes 1048576 | tf_op jit(solution)/shard_map/all_to_all | solution.py:121
  73.5 16.7 %all-to-all-done.2 = bf16[64,16,256]{2,1,0:T(8,128)(2,1)} async-done(((bf16[64,16,256]{2,1,0:T(8,128)(2,1)}), bf16[64,16,256]{2,1,0:T(8,128)(2,1)}, u32[]{:S(2)}, u32[]{:S(2)}) %all-to-all-start.2) | async-done | bytes 524320 | tf_op jit(solution)/shard_map/all_to_all | solution.py:121
  90.3 1.2 convert.23
  91.4 2.4 fusion.61
  93.8 2.4 fusion.65
  96.2 2.4 fusion.7
  98.6 3.8 %multiply_subtract_fusion = (f32[2,32,16,256]{3,1,2,0:T(8,128)S(1)}, f32[2,32,16,256]{3,1,2,0:T(8,128)}) fusion(f32[2,32,16,256]{3,1,2,0:T(8,128)S(1)} %fusion.7, f32[32,16]{0,1:T(8,128)S(1)} %get-tuple-element.30, f32[32,16]{0,1:T(8,128)S(1)} %get-tuple-element.31, f32[2,16,256,32]{2,3,1,0:T(8,128)S(1)} %fusion.61, f32[32,2,16,256]{3,2,1,0:T(8,128)S(1)} %convert.23, ...), kind=kOutput, calls=%fused_computation.60 | convolution fusion | flops 103299072 | bytes 6303744 | tf_op jit(solution)/shard_map/ab,ebcd->eacd/dot_general | solution.py:23
  102.5 4.3 %fusion.58 = (bf16[512,128]{1,0:T(8,128)(2,1)}, f32[512,128]{1,0:T(8,128)}) fusion(bf16[1,512,128]{2,1,0:T(8,128)(2,1)S(1)} %copy-done.5, bf16[128,4096]{1,0:T(8,128)(2,1)S(1)} %copy-done, bf16[1,512,4096]{2,1,0:T(8,128)(2,1)} %all-gather.4.cloned.1.call-done), kind=kOutput, calls=%fused_computation.116 | convolution fusion | flops 537067520 | bytes 5767168 | tf_op jit(solution)/shard_map/dot_general | solution.py:183
  106.8 7.4 %all-to-all-start.6 = ((bf16[32,16,128]{2,1,0:T(8,128)(2,1)}), bf16[32,16,128]{2,1,0:T(8,128)(2,1)S(1)}, u32[]{:S(2)}, u32[]{:S(2)}) async-start(bf16[32,16,128]{2,1,0:T(8,128)(2,1)} %bitcast.55), calls=%async_computation.7 | async-start | bytes 262144 | tf_op jit(solution)/shard_map/all_to_all | solution.py:105
  114.2 2.6 fusion.34
  116.8 10.0 %all-to-all-done.6 = bf16[32,16,128]{2,1,0:T(8,128)(2,1)S(1)} async-done(((bf16[32,16,128]{2,1,0:T(8,128)(2,1)}), bf16[32,16,128]{2,1,0:T(8,128)(2,1)S(1)}, u32[]{:S(2)}, u32[]{:S(2)}) %all-to-all-start.6) | async-done | bytes 131104 | tf_op jit(solution)/shard_map/all_to_all | solution.py:105
  127.3 0.9 copy.96
  128.2 4.6 %all-to-all-start.7 = ((bf16[64,16,128]{2,1,0:T(8,128)(2,1)}), bf16[64,16,128]{2,1,0:T(8,128)(2,1)}, u32[]{:S(2)}, u32[]{:S(2)}) async-start(bf16[64,16,128]{2,1,0:T(8,128)(2,1)} %copy.96), calls=%async_computation.8 | async-start | bytes 524288 | tf_op jit(solution)/shard_map/all_to_all | solution.py:118
  132.8 3.9 %fusion.5 = f32[2,32,16,256]{3,2,1,0:T(8,128)} fusion(f32[2,32,256,16]{2,3,1,0:T(8,128)} %fusion.34, f32[2,32,16,256]{3,1,2,0:T(8,128)S(1)} %copy-done.1), kind=kOutput, calls=%fused_computation.12 | convolution fusion | flops 50597376 | bytes 3145728 | tf_op jit(solution)/shard_map/ab,ecbd->ecad/dot_general | solution.py:23
  137.2 0.9 copy.99
  138.1 8.6 %all-to-all-done.7 = bf16[64,16,128]{2,1,0:T(8,128)(2,1)} async-done(((bf16[64,16,128]{2,1,0:T(8,128)(2,1)}), bf16[64,16,128]{2,1,0:T(8,128)(2,1)}, u32[]{:S(2)}, u32[]{:S(2)}) %all-to-all-start.7) | async-done | bytes 262176 | tf_op jit(solution)/shard_map/all_to_all | solution.py:118
  146.7 5.6 %all-to-all-start.8 = ((bf16[64,16,128]{2,1,0:T(8,128)(2,1)}), bf16[64,16,128]{2,1,0:T(8,128)(2,1)S(1)}, u32[]{:S(2)}, u32[]{:S(2)}) async-start(bf16[64,16,128]{2,1,0:T(8,128)(2,1)} %copy.99), calls=%async_computation.9 | async-start | bytes 524288 | tf_op jit(solution)/shard_map/all_to_all | solution.py:121
  152.3 1.6 fusion.30
  153.9 2.6 fusion.4
  156.5 1.0 convert.24
  157.5 8.6 %all-to-all-done.8 = bf16[64,16,128]{2,1,0:T(8,128)(2,1)S(1)} async-done(((bf16[64,16,128]{2,1,0:T(8,128)(2,1)}), bf16[64,16,128]{2,1,0:T(8,128)(2,1)S(1)}, u32[]{:S(2)}, u32[]{:S(2)}) %all-to-all-start.8) | async-done | bytes 262176 | tf_op jit(solution)/shard_map/all_to_all | solution.py:121
  166.2 1.3 fusion.72
  167.5 1.3 fusion.76
  168.8 1.3 fusion.12
  170.1 1.5 multiply_subtract_fusion.3
  171.6 0.9 fusion.48
  172.5 0.9 fusion.44
  173.4 0.9 fusion.9
  174.3 1.4 multiply_subtract_fusion.2
  182.2 1.0 fusion.43
  183.2 1.0 copy.91
  184.2 5.6 %all-to-all-start.4 = ((bf16[2,512,128]{2,0,1:T(2,128)(2,1)}), bf16[2,512,128]{2,0,1:T(2,128)(2,1)S(1)}, u32[]{:S(2)}, u32[]{:S(2)}) async-start(bf16[2,512,128]{2,0,1:T(2,128)(2,1)} %copy.91), calls=%async_computation.4 | async-start | bytes 524288 | tf_op jit(solution)/shard_map/all_to_all | solution.py:139
  189.8 1.9 copy.88
  191.7 11.9 %all-to-all-done.4 = bf16[2,512,128]{2,0,1:T(2,128)(2,1)S(1)} async-done(((bf16[2,512,128]{2,0,1:T(2,128)(2,1)}), bf16[2,512,128]{2,0,1:T(2,128)(2,1)S(1)}, u32[]{:S(2)}, u32[]{:S(2)}) %all-to-all-start.4) | async-done | bytes 262176 | tf_op jit(solution)/shard_map/all_to_all | solution.py:139
  203.7 5.7 %all-to-all-start.3 = ((bf16[2,512,128]{2,0,1:T(2,128)(2,1)}), bf16[2,512,128]{2,0,1:T(2,128)(2,1)}, u32[]{:S(2)}, u32[]{:S(2)}) async-start(bf16[2,512,128]{2,0,1:T(2,128)(2,1)} %copy.88), calls=%async_computation.3 | async-start | bytes 524288 | tf_op jit(solution)/shard_map/all_to_all | solution.py:136
  209.8 13.5 %all-to-all-done.3 = bf16[2,512,128]{2,0,1:T(2,128)(2,1)} async-done(((bf16[2,512,128]{2,0,1:T(2,128)(2,1)}), bf16[2,512,128]{2,0,1:T(2,128)(2,1)}, u32[]{:S(2)}, u32[]{:S(2)}) %all-to-all-start.3) | async-done | bytes 262176 | tf_op jit(solution)/shard_map/all_to_all | solution.py:136
  223.2 1.0 copy.89
  225.3 18.0 %all_to_all.129 = bf16[32,16,128]{2,1,0:T(8,128)(2,1)S(1)} all-to-all(bf16[32,16,128]{2,1,0:T(8,128)(2,1)S(1)} %copy.94), channel_id=1, replica_groups=mesh['dp'=4,'seq'=32,'tensor'=4] {'seq'}, dimensions={0} | all-to-all | bytes 262144 | tf_op jit(solution)/shard_map/all_to_all | solution.py:150
  243.3 3.2 convolution_convert_fusion
  246.5 1.1 fusion.36
  247.6 1.1 fusion.37
  248.6 1.1 convolution_add_fusion.1
  249.7 1.4 add_bitcast_fusion
  251.1 1.7 fusion.24
  252.9 1.7 fusion.2
  255.2 1.7 fusion.28
  257.0 2.0 fusion.3
  259.9 1.4 copy.116
  261.3 4.1 %all-to-all-start.10 = ((bf16[2,512,256]{2,0,1:T(2,128)(2,1)}), bf16[2,512,256]{2,0,1:T(2,128)(2,1)S(1)}, u32[]{:S(2)}, u32[]{:S(2)}) async-start(bf16[2,512,256]{2,0,1:T(2,128)(2,1)} %copy.116), calls=%async_computation.11 | async-start | bytes 1048576 | tf_op jit(solution)/shard_map/all_to_all | solution.py:139
  265.4 1.3 copy.113
  266.7 16.7 %all-to-all-done.10 = bf16[2,512,256]{2,0,1:T(2,128)(2,1)S(1)} async-done(((bf16[2,512,256]{2,0,1:T(2,128)(2,1)}), bf16[2,512,256]{2,0,1:T(2,128)(2,1)S(1)}, u32[]{:S(2)}, u32[]{:S(2)}) %all-to-all-start.10) | async-done | bytes 524320 | tf_op jit(solution)/shard_map/all_to_all | solution.py:139
  283.4 7.0 %all-to-all-start.9 = ((bf16[2,512,256]{2,0,1:T(2,128)(2,1)}), bf16[2,512,256]{2,0,1:T(2,128)(2,1)S(1)}, u32[]{:S(2)}, u32[]{:S(2)}) async-start(bf16[2,512,256]{2,0,1:T(2,128)(2,1)} %copy.113), calls=%async_computation.10 | async-start | bytes 1048576 | tf_op jit(solution)/shard_map/all_to_all | solution.py:136
  291.3 17.2 %all-to-all-done.9 = bf16[2,512,256]{2,0,1:T(2,128)(2,1)S(1)} async-done(((bf16[2,512,256]{2,0,1:T(2,128)(2,1)}), bf16[2,512,256]{2,0,1:T(2,128)(2,1)S(1)}, u32[]{:S(2)}, u32[]{:S(2)}) %all-to-all-start.9) | async-done | bytes 524320 | tf_op jit(solution)/shard_map/all_to_all | solution.py:136
  310.2 0.9 copy.119
  311.1 7.0 %all-to-all-start.11 = ((bf16[32,16,256]{2,1,0:T(8,128)(2,1)}), bf16[32,16,256]{2,1,0:T(8,128)(2,1)S(1)}, u32[]{:S(2)}, u32[]{:S(2)}) async-start(bf16[32,16,256]{2,1,0:T(8,128)(2,1)} %copy.119), calls=%async_computation.12 | async-start | bytes 524288 | tf_op jit(solution)/shard_map/all_to_all | solution.py:150
  318.8 13.2 %all-to-all-done.11 = bf16[32,16,256]{2,1,0:T(8,128)(2,1)S(1)} async-done(((bf16[32,16,256]{2,1,0:T(8,128)(2,1)}), bf16[32,16,256]{2,1,0:T(8,128)(2,1)S(1)}, u32[]{:S(2)}, u32[]{:S(2)}) %all-to-all-start.11) | async-done | bytes 262176 | tf_op jit(solution)/shard_map/all_to_all | solution.py:150
  332.7 19.2 %all-gather.1 = bf16[2048,128]{1,0:T(8,128)(2,1)S(1)} all-gather(bf16[512,128]{1,0:T(8,128)(2,1)S(1)} %get-tuple-element.22), channel_id=3, replica_groups=mesh['dp'=4,'seq'=32,'tensor'=4] {'dp'}, dimensions={0}, use_global_device_ids=true | all-gather | bytes 655360 | tf_op jit(solution)/shard_map/all_gather | solution.py:201
  (76 shorter events, 18.4 us)
Async XLA Ops:
  7.2 95.3 %copy-start = (bf16[128,4096]{1,0:T(8,128)(2,1)S(1)}, bf16[128,4096]{1,0:T(8,128)(2,1)}, u32[]{:S(2)}) copy-start(bf16[128,4096]{1,0:T(8,128)(2,1)} %param.8) | copy-start | bytes 3145732
  7.2 95.3 %all-gather.4.cloned.1.call-start = ((), (), s32[]{:S(2)}) async-start(), calls=%async_computation.14 | async-start | bytes 5242880 | tf_op jit(solution)/shard_map/all_gather | solution.py:184
  41.4 23.3 %all-to-all-start.1 = ((bf16[64,16,256]{2,1,0:T(8,128)(2,1)}), bf16[64,16,256]{2,1,0:T(8,128)(2,1)S(1)}, u32[]{:S(2)}, u32[]{:S(2)}) async-start(bf16[64,16,256]{2,1,0:T(8,128)(2,1)} %copy.71), calls=%async_computation.1 | async-start | bytes 1048576 | tf_op jit(solution)/shard_map/all_to_all | solution.py:118
  64.7 25.5 %all-to-all-start.2 = ((bf16[64,16,256]{2,1,0:T(8,128)(2,1)}), bf16[64,16,256]{2,1,0:T(8,128)(2,1)}, u32[]{:S(2)}, u32[]{:S(2)}) async-start(bf16[64,16,256]{2,1,0:T(8,128)(2,1)} %copy.74), calls=%async_computation.2 | async-start | bytes 1048576 | tf_op jit(solution)/shard_map/all_to_all | solution.py:121
  72.5 105.1 %copy-start.7 = (f32[32,16]{1,0:T(8,128)}, f32[32,16]{1,0:T(8,128)S(1)}, u32[]{:S(2)}) copy-start(f32[32,16]{1,0:T(8,128)S(1)} %copy.80) | copy-start | bytes 6148
  98.6 3.9 %copy-start.5 = (bf16[1,512,128]{2,1,0:T(8,128)(2,1)S(1)}, bf16[1,512,128]{2,1,0:T(8,128)(2,1)}, u32[]{:S(2)}) copy-start(bf16[1,512,128]{2,1,0:T(8,128)(2,1)} %param.5) | copy-start | bytes 393220
  102.5 30.3 %copy-start.1 = (f32[2,32,16,256]{3,1,2,0:T(8,128)S(1)}, f32[2,32,16,256]{3,1,2,0:T(8,128)}, u32[]{:S(2)}) copy-start(f32[2,32,16,256]{3,1,2,0:T(8,128)} %get-tuple-element.11) | copy-start | bytes 3145732
  106.8 20.0 %all-to-all-start.6 = ((bf16[32,16,128]{2,1,0:T(8,128)(2,1)}), bf16[32,16,128]{2,1,0:T(8,128)(2,1)S(1)}, u32[]{:S(2)}, u32[]{:S(2)}) async-start(bf16[32,16,128]{2,1,0:T(8,128)(2,1)} %bitcast.55), calls=%async_computation.7 | async-start | bytes 262144 | tf_op jit(solution)/shard_map/all_to_all | solution.py:105
  128.2 18.5 %all-to-all-start.7 = ((bf16[64,16,128]{2,1,0:T(8,128)(2,1)}), bf16[64,16,128]{2,1,0:T(8,128)(2,1)}, u32[]{:S(2)}, u32[]{:S(2)}) async-start(bf16[64,16,128]{2,1,0:T(8,128)(2,1)} %copy.96), calls=%async_computation.8 | async-start | bytes 524288 | tf_op jit(solution)/shard_map/all_to_all | solution.py:118
  146.7 19.5 %all-to-all-start.8 = ((bf16[64,16,128]{2,1,0:T(8,128)(2,1)}), bf16[64,16,128]{2,1,0:T(8,128)(2,1)S(1)}, u32[]{:S(2)}, u32[]{:S(2)}) async-start(bf16[64,16,128]{2,1,0:T(8,128)(2,1)} %copy.99), calls=%async_computation.9 | async-start | bytes 524288 | tf_op jit(solution)/shard_map/all_to_all | solution.py:121
  168.8 5.5 %copy-start.2 = (f32[2,32,16,256]{3,2,1,0:T(8,128)S(1)}, f32[2,32,16,256]{3,2,1,0:T(8,128)}, u32[]{:S(2)}) copy-start(f32[2,32,16,256]{3,2,1,0:T(8,128)} %fusion.5) | copy-start | bytes 3145732
  168.8 5.5 %copy-start.3 = (f32[2,32,16,256]{3,2,1,0:T(8,128)S(1)}, f32[2,32,16,256]{3,2,1,0:T(8,128)}, u32[]{:S(2)}) copy-start(f32[2,32,16,256]{3,2,1,0:T(8,128)} %fusion.4) | copy-start | bytes 3145732
  178.4 3.8 %copy-start.9 = (f32[2,512]{1,0:T(2,128)S(1)}, f32[2,512]{1,0:T(2,128)}, u32[]{:S(2)}) copy-start(f32[2,512]{1,0:T(2,128)} %get-tuple-element.26) | copy-start | bytes 12292
  178.4 3.8 %copy-start.11 = (f32[2,512]{1,0:T(2,128)S(1)}, f32[2,512]{1,0:T(2,128)}, u32[]{:S(2)}) copy-start(f32[2,512]{1,0:T(2,128)} %get-tuple-element.27) | copy-start | bytes 12292
  181.8 61.4 %copy-start.6 = (bf16[1,512,128]{2,1,0:T(8,128)(2,1)S(1)}, bf16[1,512,128]{2,1,0:T(8,128)(2,1)}, u32[]{:S(2)}) copy-start(bf16[1,512,128]{2,1,0:T(8,128)(2,1)} %param.5) | copy-start | bytes 393220
  184.2 19.5 %all-to-all-start.4 = ((bf16[2,512,128]{2,0,1:T(2,128)(2,1)}), bf16[2,512,128]{2,0,1:T(2,128)(2,1)S(1)}, u32[]{:S(2)}, u32[]{:S(2)}) async-start(bf16[2,512,128]{2,0,1:T(2,128)(2,1)} %copy.91), calls=%async_computation.4 | async-start | bytes 524288 | tf_op jit(solution)/shard_map/all_to_all | solution.py:139
  203.7 19.6 %all-to-all-start.3 = ((bf16[2,512,128]{2,0,1:T(2,128)(2,1)}), bf16[2,512,128]{2,0,1:T(2,128)(2,1)}, u32[]{:S(2)}, u32[]{:S(2)}) async-start(bf16[2,512,128]{2,0,1:T(2,128)(2,1)} %copy.88), calls=%async_computation.3 | async-start | bytes 524288 | tf_op jit(solution)/shard_map/all_to_all | solution.py:136
  209.4 143.3 %reduce-scatter.2.cloned.1.call-start = ((), (), s32[]{:S(2)}) async-start(), calls=%async_computation.13 | async-start | bytes 5242880 | tf_op jit(solution)/shard_map/reduce_scatter | solution.py:180
  246.5 3.2 copy-start.8
  255.2 4.3 %copy-start.10 = (f32[2,512]{1,0:T(2,128)S(1)}, f32[2,512]{1,0:T(2,128)}, u32[]{:S(2)}) copy-start(f32[2,512]{1,0:T(2,128)} %get-tuple-element.26) | copy-start | bytes 12292
  255.2 4.3 %copy-start.12 = (f32[2,512]{1,0:T(2,128)S(1)}, f32[2,512]{1,0:T(2,128)}, u32[]{:S(2)}) copy-start(f32[2,512]{1,0:T(2,128)} %get-tuple-element.27) | copy-start | bytes 12292
  261.3 22.1 %all-to-all-start.10 = ((bf16[2,512,256]{2,0,1:T(2,128)(2,1)}), bf16[2,512,256]{2,0,1:T(2,128)(2,1)S(1)}, u32[]{:S(2)}, u32[]{:S(2)}) async-start(bf16[2,512,256]{2,0,1:T(2,128)(2,1)} %copy.116), calls=%async_computation.11 | async-start | bytes 1048576 | tf_op jit(solution)/shard_map/all_to_all | solution.py:139
  283.4 25.1 %all-to-all-start.9 = ((bf16[2,512,256]{2,0,1:T(2,128)(2,1)}), bf16[2,512,256]{2,0,1:T(2,128)(2,1)S(1)}, u32[]{:S(2)}, u32[]{:S(2)}) async-start(bf16[2,512,256]{2,0,1:T(2,128)(2,1)} %copy.113), calls=%async_computation.10 | async-start | bytes 1048576 | tf_op jit(solution)/shard_map/all_to_all | solution.py:136
  290.5 27.6 %copy-start.4 = (f32[512,128]{1,0:T(8,128)S(1)}, f32[512,128]{1,0:T(8,128)}, u32[]{:S(2)}) copy-start(f32[512,128]{1,0:T(8,128)} %get-tuple-element.29) | copy-start | bytes 786436
  311.1 20.9 %all-to-all-start.11 = ((bf16[32,16,256]{2,1,0:T(8,128)(2,1)}), bf16[32,16,256]{2,1,0:T(8,128)(2,1)S(1)}, u32[]{:S(2)}, u32[]{:S(2)}) async-start(bf16[32,16,256]{2,1,0:T(8,128)(2,1)} %copy.119), calls=%async_computation.12 | async-start | bytes 524288 | tf_op jit(solution)/shard_map/all_to_all | solution.py:150
Sparse Core Ops, SparseCore 0:
  10.1 57.5 all-gather.3
  246.6 46.3 reduce-scatter.1
